TPU v7x, 32 devices: a whole 2x2x4 slice. The times are simulated.
32 devices in a mesh: wa: 4 (over z), ha: 8 (over y, x, core).
Axes of the slice: x: 2, y: 2, z: 4, core: 2. Of those that a mesh axis runs over, the one named last changes fastest.
Arguments:
- tokens: bfloat16 [1024, 16384], P('ha', 'wa'), may hold values from -6 to 6
- gain_attn: bfloat16 [16384], P('wa'), may hold values from 0.25 to 1.75
- w_query: bfloat16 [16384, 16384], P('wa', 'ha'), may hold values from -0.046875 to 0.046875, as said below
- w_key: bfloat16 [16384, 1024], P('wa'), may hold values from -1.171875 to 1.171875, as said below
- w_value: bfloat16 [16384, 1024], P('wa'), may hold values from -0.046875 to 0.046875
- w_out: bfloat16 [16384, 16384], P('ha', 'wa'), may hold values from -0.1875 to 0.1875
- gain_ffn: bfloat16 [16384], P('wa'), may hold values from 0.25 to 1.75
- segment_ids: int32 [1024], replicated, may hold values from 0 to 31, never falling along the last dimension, each value on 1 to 256 neighbouring positions
Outputs:
- residual_out: bfloat16 [1024, 16384], P('ha', 'wa')
- ffn_input: bfloat16 [1024, 16384], P('ha', 'wa')
Inputs may be any that keep to these rules, and one draw needn't show every extreme that they name: `w_query`: entries scaled by 16384 ** -0.5. `w_key`: entries scaled by 16384 ** -0.5. `segment_ids`: segment ids never fall along the tokens; each prompt has 1 to 256 tokens and one has exactly 256.
All inputs are finite; a program needn't handle non-finite values.
Results may differ from a plain program's by a relative error of at most 0.00675.
The roundings to bfloat16 on the way count: a program that leaves them out, or rounds other values in their place, can miss the bound.
Values may be sent and summed in bfloat16 or wider, within the bound.
A program may use at most 192 MiB of HBM per device.

v0:
```python
import jax
import jax.numpy as jnp
from jax import lax
from jax.sharding import PartitionSpec as P

KVH = 8
HD = 128
EPS = 1e-05


def rope_tables(position):
    half = HD // 2
    inverse = 500000.0 ** (-(jnp.arange(half, dtype=jnp.float32) * 2.0 / HD))
    angle = position[:, None] * inverse[None, :]
    return (jnp.cos(angle), jnp.sin(angle))


def rotate(values, cosine, sine):
    half = values.shape[-1] // 2
    first = values[..., :half]
    second = values[..., half:]
    cosine = cosine[:, None, :]
    sine = sine[:, None, :]
    return jnp.concatenate(
        [first * cosine - second * sine, second * cosine + first * sine], axis=-1
    )


def on_device(tokens, gain_attn, w_query, w_key, w_value, w_out, gain_ffn, segment_ids):
    rows_dev, width_dev = tokens.shape
    n_wa = lax.axis_size("wa")
    n_ha = lax.axis_size("ha")
    total = rows_dev * n_ha
    width = width_dev * n_wa
    head_cols = w_query.shape[1]
    heads_dev = head_cols // HD
    token_f = tokens.astype(jnp.float32)
    gain_one = gain_attn.astype(jnp.float32)
    kv_head = lax.axis_index("ha") // (n_ha // KVH)
    kv_weights = jnp.concatenate(
        [
            lax.dynamic_slice_in_dim(w_key, kv_head * HD, HD, 1),
            lax.dynamic_slice_in_dim(w_value, kv_head * HD, HD, 1),
        ],
        axis=1,
    )
    gathered = lax.all_gather(tokens, "ha", axis=0, tiled=True)
    own_sq = lax.psum(jnp.sum(token_f * token_f, axis=1), "wa")
    own_scale = lax.rsqrt(own_sq / width + EPS)
    row_scale = lax.all_gather(own_scale, "ha", axis=0, tiled=True)
    scaled = (gathered.astype(jnp.float32) * gain_one).astype(jnp.bfloat16)
    kv_part = jnp.dot(scaled, kv_weights, preferred_element_type=jnp.float32)
    kv_sum = lax.psum(kv_part, "wa")
    index_all = jnp.arange(total, dtype=jnp.int32)
    fresh = jnp.concatenate([jnp.ones((1,), dtype=bool), segment_ids[1:] != segment_ids[:-1]])
    start_all = lax.cummax(jnp.where(fresh, index_all, jnp.zeros_like(index_all)), axis=0)
    cosine, sine = rope_tables((index_all - start_all).astype(jnp.float32))
    key_plain = (kv_sum[:, :HD] * row_scale[:, None]).astype(jnp.bfloat16)
    key_plain = lax.optimization_barrier(key_plain)
    value_head = (kv_sum[:, HD:] * row_scale[:, None]).astype(jnp.bfloat16)
    key_head = rotate(key_plain.astype(jnp.float32).reshape(total, 1, HD), cosine, sine)
    key_head = key_head.reshape(total, HD).astype(jnp.bfloat16)
    q_rows = total // n_wa
    first = lax.axis_index("wa") * q_rows
    block = scaled
    query_f = lax.psum_scatter(
        jnp.dot(block, w_query, preferred_element_type=jnp.float32),
        "wa",
        scatter_dimension=0,
        tiled=True,
    )
    q_scale = lax.dynamic_slice_in_dim(row_scale, first, q_rows, 0)
    q_cos = lax.dynamic_slice_in_dim(cosine, first, q_rows, 0)
    q_sin = lax.dynamic_slice_in_dim(sine, first, q_rows, 0)
    queries = rotate(
        (query_f * q_scale[:, None]).reshape(q_rows, heads_dev, HD), q_cos, q_sin
    ).astype(jnp.bfloat16)
    q_segment = lax.dynamic_slice_in_dim(segment_ids, first, q_rows, 0)
    q_index = first + jnp.arange(q_rows, dtype=jnp.int32)
    allowed = (q_segment[:, None] == segment_ids[None, :]) & (
        index_all[None, :] <= q_index[:, None]
    )
    scores = jnp.einsum(
        "thd,sd->hts", queries, key_head, preferred_element_type=jnp.float32
    ) * HD ** (-0.5)
    scores = jnp.where(allowed[None], scores, -1e30)
    peak = jnp.max(scores, axis=-1, keepdims=True)
    expo = jnp.where(allowed[None], jnp.exp(scores - peak), 0.0)
    weights = (expo / jnp.sum(expo, axis=-1, keepdims=True)).astype(jnp.bfloat16)
    head_out = jnp.einsum("hts,sd->thd", weights, value_head, preferred_element_type=jnp.float32)
    head_out = head_out.astype(jnp.bfloat16).reshape(q_rows, head_cols)
    head_all = lax.all_gather(head_out, "wa", axis=0, tiled=True)
    block = head_all
    attended = lax.psum_scatter(
        jnp.dot(block, w_out, preferred_element_type=jnp.float32),
        "ha",
        scatter_dimension=0,
        tiled=True,
    )
    residual_out = (token_f + attended).astype(jnp.bfloat16)
    residual_f = residual_out.astype(jnp.float32)
    square_two = lax.psum(jnp.sum(residual_f * residual_f, axis=1), "wa")
    scale_two = lax.rsqrt(square_two / width + EPS)
    ffn_input = (residual_f * scale_two[:, None] * gain_ffn.astype(jnp.float32)).astype(
        jnp.bfloat16
    )
    return (residual_out, ffn_input)


def solution(mesh):
    in_specs = (
        P("ha", "wa"),
        P("wa"),
        P("wa", "ha"),
        P("wa", None),
        P("wa", None),
        P("ha", "wa"),
        P("wa"),
        P(),
    )
    out_specs = (P("ha", "wa"), P("ha", "wa"))
    return jax.shard_map(
        on_device, mesh=mesh, in_specs=in_specs, out_specs=out_specs, check_vma=False
    )
```

profile of v0, /device:TPU:0, one launch (start us, length us, event | category | flops | bytes accessed | tf_op | source)
XLA Modules:
  0.0 537.4 jit_solution(1475122119710769772)
XLA Ops:
  7.2 0.7 all-gather.4.cloned.1.call-update
  7.9 0.7 convert_element_type.54
  8.6 1.7 constant_dynamic-slice_fusion
  10.3 56.5 %all-gather.4.cloned.1.call-done = bf16[1024,4096]{1,0:T(8,128)(2,1)} async-done(((bf16[128,4096]{1,0:T(8,128)(2,1)}), bf16[1024,4096]{1,0:T(8,128)(2,1)}) %all-gather.4.cloned.1.call-update) | async-done | bytes 8388624 | tf_op jit(solution)/shard_map/all_gather | solution.py:47
  66.9 6.7 %fusion.7 = f32[1024,256]{0,1:T(8,128)} fusion(bf16[1024,4096]{1,0:T(8,128)(2,1)} %all-gather.4.cloned.1.call-done, f32[4096]{0:T(1024)S(1)} %convert_element_type.54, bf16[4096,128]{1,0:T(8,128)(2,1)S(1)} %get-tuple-element.14, bf16[4096,128]{1,0:T(8,128)(2,1)S(1)} %get-tuple-element.15), kind=kOutput, calls=%fused_computation.11 | convolution fusion | flops 2164260864 | bytes 11550720 | tf_op jit(solution)/shard_map/dot_general | solution.py:52
  73.7 24.0 %fusion.6 = f32[1024,2048]{1,0:T(8,128)} fusion(bf16[4096,2048]{1,0:T(8,128)(2,1)} %param.10, bf16[1024,4096]{1,0:T(8,128)(2,1)} %all-gather.4.cloned.1.call-done, f32[4096]{0:T(1024)S(1)} %convert_element_type.54), kind=kOutput, calls=%fused_computation.10 | convolution fusion | flops 17192452096 | bytes 33570816 | tf_op jit(solution)/shard_map/dot_general | solution.py:67
  97.8 1.1 copy-done
  98.9 0.3 fusion.8
  99.2 11.7 %psum.22 = f32[128]{0:T(128)S(1)} all-reduce(f32[128]{0:T(128)S(1)} %fusion.8), channel_id=1, replica_groups=mesh['wa'=4,'ha'=8] {'wa'}, use_global_device_ids=true, to_apply=%region_2.3 | all-reduce | flops 128 | bytes 1024 | tf_op jit(solution)/shard_map/psum | solution.py:48
  111.0 8.9 %all-gather = f32[8,1,128]{2,1,0:T(1,128)S(1)} all-gather(f32[1,1,128]{2,1,0:T(1,128)S(1)} %rsqrt_bitcast_fusion), channel_id=1, replica_groups=mesh['wa'=4,'ha'=8] {'ha'}, dimensions={0}, use_global_device_ids=true | all-gather | bytes 4608 | tf_op jit(solution)/shard_map/all_gather | solution.py:50
  120.1 0.3 reduce-window.9
  120.7 0.2 broadcast_multiply_fusion
  121.0 0.5 dynamic-slice_cosine_fusion
  121.4 1.0 fusion.19
  122.4 3.3 all-reduce.2.cloned.1.call-done
  125.7 1.1 fusion.20
  126.8 1.8 fusion.27
  128.6 143.4 %reduce-scatter.3.cloned.1.call-done = f32[256,2048]{1,0:T(8,128)} async-done(((f32[1024,2048]{1,0:T(8,128)}), f32[256,2048]{1,0:T(8,128)}) %reduce-scatter.3.cloned.1.call-update) | async-done | bytes 2097168 | tf_op jit(solution)/shard_map/reduce_scatter | solution.py:66
  272.0 1.8 multiply_bitcast_fusion
  273.8 0.4 copy.33
  274.2 0.7 fusion.43
  274.9 1.4 subtract_convert_fusion
  276.2 11.8 %fusion.44 = (f32[16,256]{1,0:T(8,128)S(1)}, f32[16,256,1024]{1,2,0:T(8,128)}) fusion(pred[256,1024]{0,1:T(8,128)(4,1)} %fusion.19, bf16[1024,1,64]{0,2,1:T(8,128)(2,1)} %get-tuple-element.9, bf16[1024,1,64]{0,2,1:T(8,128)(2,1)S(1)} %get-tuple-element.8, bf16[256,16,64]{2,0,1:T(8,128)(2,1)S(1)} %get-tuple-element.5, ...), kind=kOutput, calls=%fused_computation.72 | convolution fusion | flops 1097335808 | bytes 18366464 | tf_op jit(solution)/shard_map/sub | solution.py:88
  288.0 8.2 %fusion.18 = bf16[128,16,256]{2,0,1:T(8,128)(2,1)} fusion(f32[16,256,1024]{1,2,0:T(8,128)} %get-tuple-element.13, f32[16,256]{1,0:T(8,128)S(1)} %get-tuple-element.12, f32[1024,256]{0,1:T(8,128)} %all-reduce.2.cloned.1.call-done, f32[1024]{0:T(1024)S(1)} %bitcast.55), kind=kOutput, calls=%fused_computation.28 | convolution fusion | flops 1082916864 | bytes 18370560 | tf_op jit(solution)/shard_map/hts,sd->thd/dot_general | solution.py:90
  296.3 0.3 reduce-scatter.5.cloned.1.call-start
  296.6 81.0 %all-gather.6.cloned.1.call-done = bf16[1024,2048]{0,1:T(8,128)(2,1)} async-done(((bf16[256,2048]{0,1:T(8,128)(2,1)}), bf16[1024,2048]{0,1:T(8,128)(2,1)}) %all-gather.6.cloned.1.call-update) | async-done | bytes 4194320 | tf_op jit(solution)/shard_map/all_gather | solution.py:92
  377.6 23.7 %fusion.45 = f32[1024,4096]{1,0:T(8,128)} fusion(bf16[1024,2048]{0,1:T(8,128)(2,1)} %all-gather.6.cloned.1.call-done, bf16[2048,4096]{1,0:T(8,128)(2,1)} %param.13), kind=kOutput, calls=%fused_computation.73 | convolution fusion | flops 17179869184 | bytes 37748736 | tf_op jit(solution)/shard_map/dot_general | solution.py:95
  401.4 0.7 copy-done.3
  402.0 113.9 %reduce-scatter.5.cloned.1.call-done = f32[128,4096]{1,0:T(8,128)} async-done(((f32[1024,4096]{1,0:T(8,128)}), f32[128,4096]{1,0:T(8,128)}) %reduce-scatter.5.cloned.1.call-update) | async-done | bytes 2097168 | tf_op jit(solution)/shard_map/reduce_scatter | solution.py:94
  515.9 2.0 fusion.10
  517.9 11.7 %psum.23 = f32[128]{0:T(128)S(1)} all-reduce(f32[128]{0:T(128)S(1)} %get-tuple-element.2), channel_id=1, replica_groups=mesh['wa'=4,'ha'=8] {'wa'}, use_global_device_ids=true, to_apply=%region_10.11 | all-reduce | flops 128 | bytes 1024 | tf_op jit(solution)/shard_map/psum | solution.py:102
  529.6 1.3 fusion.12
  (28 shorter events, 0.9 us)
Async XLA Ops:
  7.2 59.7 %all-gather.4.cloned.1.call-start = ((), (), s32[]{:S(2)}) async-start(), calls=%async_computation.2 | async-start | bytes 9437184 | tf_op jit(solution)/shard_map/all_gather | solution.py:47
  7.9 117.8 %all-reduce.2.cloned.1.call-start = ((), (), s32[]{:S(2)}) async-start(), calls=%async_computation.3 | async-start | bytes 2097152 | tf_op jit(solution)/shard_map/psum | solution.py:53
  73.6 198.4 %reduce-scatter.3.cloned.1.call-start = ((), (), s32[]{:S(2)}) async-start(), calls=%async_computation.4 | async-start | bytes 10485760 | tf_op jit(solution)/shard_map/reduce_scatter | solution.py:66
  97.7 1.2 copy-start
  97.7 22.2 %copy-start.2 = (s32[1024]{0:T(1024)S(1)}, s32[1024]{0:T(1024)}, u32[]{:S(2)}) copy-start(s32[1024]{0:T(1024)} %param.15) | copy-start | bytes 12292
  97.7 279.9 %all-gather.6.cloned.1.call-start = ((), (), s32[]{:S(2)}) async-start(), calls=%async_computation.5 | async-start | bytes 5242880 | tf_op jit(solution)/shard_map/all_gather | solution.py:92
  296.3 219.6 %reduce-scatter.5.cloned.1.call-start = ((), (), s32[]{:S(2)}) async-start(), calls=%async_computation.6 | async-start | bytes 18874368 | tf_op jit(solution)/shard_map/reduce_scatter | solution.py:94
  401.3 0.7 copy-start.3
  517.9 13.0 %copy-start.1 = (bf16[128,4096]{1,0:T(8,128)(2,1)}, bf16[128,4096]{1,0:T(8,128)(2,1)S(1)}, u32[]{:S(2)}) copy-start(bf16[128,4096]{1,0:T(8,128)(2,1)S(1)} %get-tuple-element.3) | copy-start | bytes 3145732
Sparse Core Ops, SparseCore 0:
  9.9 56.9 all-gather.3
  73.7 51.9 all-reduce.1
  128.1 143.8 reduce-scatter.2
  296.4 81.1 all-gather.5
  401.5 114.3 reduce-scatter.4
where the time goes:
time: 538 us; the launch traced here: 537 us
  waiting for transfers between devices  399 us (74%)
  matrix products  74.5 us (14%)
  blocking collectives  32.3 us (6%)
  between operations  13.9 us (3%)
  other arithmetic  12.1 us (2%)
  local copies, waits for them, and re-layouts  5.39 us (1%)
    reduce_scatter x1, waiting for transfers between devices, on_device(): lax.psum_scatter(jnp.dot(block, w_query, preferred_element_type=jnp.float...  143 us
    reduce_scatter x1, waiting for transfers between devices, on_device(): lax.psum_scatter(jnp.dot(block, w_out, preferred_element_type=jnp.float32...  114 us
    all_gather x1, waiting for transfers between devices, on_device(): head_all = lax.all_gather(head_out, 'wa', axis=0, tiled=True)  81 us
    all_gather x1, waiting for transfers between devices, on_device(): gathered = lax.all_gather(tokens, 'ha', axis=0, tiled=True)  56.5 us
    dot_general x1, matrix products, on_device(): jnp.dot(block, w_query, preferred_element_type=jnp.float32)  24 us
    dot_general x1, matrix products, on_device(): jnp.dot(block, w_out, preferred_element_type=jnp.float32)  23.7 us
    sub x1, matrix products, on_device(): expo = jnp.where(allowed[None], jnp.exp(scores - peak), 0.0)  11.8 us
    psum x1, blocking collectives, on_device(): own_sq = lax.psum(jnp.sum(token_f * token_f, axis=1), 'wa')  11.7 us
  transfers between devices with their start and end apart: 5, of which 5 were waited for; matrix products, arithmetic and copies ran while one was open for 6% of the time, Pallas kernels for 0%

commit v1 on v0

--- a/solution.py
+++ b/solution.py
@@ -89,7 +89,13 @@
     weights = (expo / jnp.sum(expo, axis=-1, keepdims=True)).astype(jnp.bfloat16)
     head_out = jnp.einsum("hts,sd->thd", weights, value_head, preferred_element_type=jnp.float32)
     head_out = head_out.astype(jnp.bfloat16).reshape(q_rows, head_cols)
-    head_all = lax.all_gather(head_out, "wa", axis=0, tiled=True)
+    size = lax.axis_size("wa")
+    held, parts = (head_out, [head_out])
+    for _ in range(size - 1):
+        held = lax.ppermute(held, "wa", [(i, (i + 1) % size) for i in range(size)])
+        parts.insert(0, held)
+    flat = jnp.concatenate(parts, axis=0)
+    head_all = jnp.roll(flat, (lax.axis_index("wa") + 1) * head_out.shape[0], axis=0)
     block = head_all
     attended = lax.psum_scatter(
         jnp.dot(block, w_out, preferred_element_type=jnp.float32),

time: 538 us -> 538 us (level)
  local copies, waits for them, and re-layouts: 5.39 us -> 11.4 us
    all_gather x1 -> x0, waiting for transfers between devices: 81 us -> none  [on_device(): head_all = lax.all_gather(head_out, 'wa', axis=0, tiled=True)]
    ppermute x0 -> x3, waiting for transfers between devices: none -> 75.7 us  [on_device(): held = lax.ppermute(held, 'wa', [(i, (i + 1) % size) for i in range(size)])]
    unnamed x9 -> x16, local copies, waits for them, and re-layouts: 2.22 us -> 8.1 us
  transfers between devices with their start and end apart: 5 -> 7, of which waited for: 5 -> 7; matrix products, arithmetic and copies ran while one was open for 6% -> 6% of each run, Pallas kernels for 0% -> 0%
where the time goes in v1:
time: 538 us; the launch traced here: 537 us
  waiting for transfers between devices  394 us (73%)
  matrix products  72.8 us (14%)
  blocking collectives  32.3 us (6%)
  between operations  13.9 us (3%)
  other arithmetic  12.1 us (2%)
  local copies, waits for them, and re-layouts  11.4 us (2%)
    reduce_scatter x1, waiting for transfers between devices, on_device(): lax.psum_scatter(jnp.dot(block, w_query, preferred_element_type=jnp.float...  143 us
    reduce_scatter x1, waiting for transfers between devices, on_device(): lax.psum_scatter(jnp.dot(block, w_out, preferred_element_type=jnp.float32...  114 us
    ppermute x3, waiting for transfers between devices, on_device(): held = lax.ppermute(held, 'wa', [(i, (i + 1) % size) for i in range(size)])  75.7 us
    all_gather x1, waiting for transfers between devices, on_device(): gathered = lax.all_gather(tokens, 'ha', axis=0, tiled=True)  56.5 us
    dot_general x1, matrix products, on_device(): jnp.dot(block, w_query, preferred_element_type=jnp.float32)  24 us
    dot_general x1, matrix products, on_device(): jnp.dot(block, w_out, preferred_element_type=jnp.float32)  22.5 us
    sub x1, matrix products, on_device(): expo = jnp.where(allowed[None], jnp.exp(scores - peak), 0.0)  12.4 us
    psum x1, blocking collectives, on_device(): own_sq = lax.psum(jnp.sum(token_f * token_f, axis=1), 'wa')  11.7 us
  transfers between devices with their start and end apart: 7, of which 7 were waited for; matrix products, arithmetic and copies ran while one was open for 6% of the time, Pallas kernels for 0%

profile of v1, /device:TPU:0, one launch (start us, length us, event | category | flops | bytes accessed | tf_op | source)
XLA Modules:
  0.0 537.3 jit_solution(8096138499343716355)
XLA Ops:
  7.2 0.7 all-gather.3.cloned.1.call-update
  7.9 0.7 convert_element_type.54
  8.6 1.7 constant_dynamic-slice_fusion
  10.3 56.5 %all-gather.3.cloned.1.call-done = bf16[1024,4096]{1,0:T(8,128)(2,1)} async-done(((bf16[128,4096]{1,0:T(8,128)(2,1)}), bf16[1024,4096]{1,0:T(8,128)(2,1)}) %all-gather.3.cloned.1.call-update) | async-done | bytes 8388624 | tf_op jit(solution)/shard_map/all_gather | solution.py:47
  66.9 6.7 %fusion.7 = f32[1024,256]{0,1:T(8,128)} fusion(bf16[1024,4096]{1,0:T(8,128)(2,1)} %all-gather.3.cloned.1.call-done, f32[4096]{0:T(1024)S(1)} %convert_element_type.54, bf16[4096,128]{1,0:T(8,128)(2,1)S(1)} %get-tuple-element.14, bf16[4096,128]{1,0:T(8,128)(2,1)S(1)} %get-tuple-element.15), kind=kOutput, calls=%fused_computation.11 | convolution fusion | flops 2164260864 | bytes 11550720 | tf_op jit(solution)/shard_map/dot_general | solution.py:52
  73.7 24.0 %fusion.6 = f32[1024,2048]{1,0:T(8,128)} fusion(bf16[4096,2048]{1,0:T(8,128)(2,1)} %param.10, bf16[1024,4096]{1,0:T(8,128)(2,1)} %all-gather.3.cloned.1.call-done, f32[4096]{0:T(1024)S(1)} %convert_element_type.54), kind=kOutput, calls=%fused_computation.10 | convolution fusion | flops 17192452096 | bytes 33570816 | tf_op jit(solution)/shard_map/dot_general | solution.py:67
  97.8 1.1 copy-done
  99.2 11.7 %psum.22 = f32[128]{0:T(128)S(1)} all-reduce(f32[128]{0:T(128)S(1)} %fusion.10), channel_id=1, replica_groups=mesh['wa'=4,'ha'=8] {'wa'}, use_global_device_ids=true, to_apply=%region_2.3 | all-reduce | flops 128 | bytes 1024 | tf_op jit(solution)/shard_map/psum | solution.py:48
  111.0 8.9 %all-gather = f32[8,1,128]{2,1,0:T(1,128)S(1)} all-gather(f32[1,1,128]{2,1,0:T(1,128)S(1)} %rsqrt_bitcast_fusion), channel_id=1, replica_groups=mesh['wa'=4,'ha'=8] {'ha'}, dimensions={0}, use_global_device_ids=true | all-gather | bytes 4608 | tf_op jit(solution)/shard_map/all_gather | solution.py:50
  121.4 1.0 fusion.21
  122.4 3.3 all-reduce.2.cloned.1.call-done
  125.7 1.1 fusion.22
  126.8 1.8 fusion.29
  128.6 143.4 %reduce-scatter.3.cloned.1.call-done = f32[256,2048]{1,0:T(8,128)} async-done(((f32[1024,2048]{1,0:T(8,128)}), f32[256,2048]{1,0:T(8,128)}) %reduce-scatter.3.cloned.1.call-update) | async-done | bytes 2097168 | tf_op jit(solution)/shard_map/reduce_scatter | solution.py:66
  272.0 1.8 multiply_bitcast_fusion
  274.2 0.7 fusion.46
  274.9 1.4 subtract_convert_fusion
  276.2 12.4 %fusion.47 = (f32[16,256]{1,0:T(8,128)}, f32[16,256,1024]{1,2,0:T(8,128)}) fusion(pred[256,1024]{0,1:T(8,128)(4,1)} %fusion.21, bf16[1024,1,64]{0,2,1:T(8,128)(2,1)} %get-tuple-element.9, bf16[1024,1,64]{0,2,1:T(8,128)(2,1)S(1)} %get-tuple-element.8, bf16[256,16,64]{2,0,1:T(8,128)(2,1)S(1)} %get-tuple-element.5, bf16[256,16,64]{2,0,1:T(8,128)(2,1)S(1)} %get-tuple-element.4), kind=kOutput, calls=%fused_computation.83 | convolution fusion | flops 1097335808 | bytes 18366464 | tf_op jit(solution)/shard_map/sub | solution.py:88
  288.6 7.1 %fusion.20 = bf16[128,16,256]{2,0,1:T(8,128)(2,1)S(1)} fusion(f32[16,256,1024]{1,2,0:T(8,128)} %get-tuple-element.13, f32[16,256]{1,0:T(8,128)} %get-tuple-element.12, f32[1024,256]{0,1:T(8,128)} %all-reduce.2.cloned.1.call-done, f32[1024]{0:T(1024)S(1)} %bitcast.56), kind=kOutput, calls=%fused_computation.30 | convolution fusion | flops 1082916864 | bytes 18370560 | tf_op jit(solution)/shard_map/hts,sd->thd/dot_general | solution.py:90
  295.8 1.1 collective-permute-start
  296.9 25.3 %collective-permute-done = bf16[256,2048]{0,1:T(8,128)(2,1)S(1)} collective-permute-done((bf16[256,2048]{0,1:T(8,128)(2,1)S(1)}, bf16[256,2048]{0,1:T(8,128)(2,1)S(1)}, u32[]{:S(2)}, u32[]{:S(2)}) %collective-permute-start) | collective-permute-done | bytes 1048608 | tf_op jit(solution)/shard_map/ppermute | solution.py:95
  322.1 25.6 %collective-permute-done.1 = bf16[256,2048]{0,1:T(8,128)(2,1)} collective-permute-done((bf16[256,2048]{0,1:T(8,128)(2,1)S(1)}, bf16[256,2048]{0,1:T(8,128)(2,1)}, u32[]{:S(2)}, u32[]{:S(2)}) %collective-permute-start.1) | collective-permute-done | bytes 1048608 | tf_op jit(solution)/shard_map/ppermute | solution.py:95
  347.7 24.9 %collective-permute-done.2 = bf16[256,2048]{0,1:T(8,128)(2,1)} collective-permute-done((bf16[256,2048]{0,1:T(8,128)(2,1)}, bf16[256,2048]{0,1:T(8,128)(2,1)}, u32[]{:S(2)}, u32[]{:S(2)}) %collective-permute-start.2) | collective-permute-done | bytes 1048608 | tf_op jit(solution)/shard_map/ppermute | solution.py:95
  372.6 1.4 constant_dynamic-update-slice_fusion.7
  374.0 1.4 constant_dynamic-update-slice_fusion.6
  375.6 1.4 constant_dynamic-update-slice_fusion.3
  377.0 1.4 constant_dynamic-update-slice_fusion.2
  378.7 22.5 %fusion.8 = f32[1024,4096]{1,0:T(8,128)} fusion(bf16[2048,4096]{1,0:T(8,128)(2,1)} %param.13, bf16[2048,2048]{0,1:T(8,128)(2,1)S(1)} %constant_dynamic-update-slice_fusion, s32[]{:T(128)S(6)} %select_n.43), kind=kOutput, calls=%fused_computation.12 | convolution fusion | flops 17179869184 | bytes 37748740 | tf_op jit(solution)/shard_map/dot_general | solution.py:101
  401.9 113.8 %reduce-scatter.5.cloned.1.call-done = f32[128,4096]{1,0:T(8,128)} async-done(((f32[1024,4096]{1,0:T(8,128)}), f32[128,4096]{1,0:T(8,128)}) %reduce-scatter.5.cloned.1.call-update) | async-done | bytes 2097168 | tf_op jit(solution)/shard_map/reduce_scatter | solution.py:100
  515.7 2.0 fusion.12
  517.7 11.7 %psum.23 = f32[128]{0:T(128)S(1)} all-reduce(f32[128]{0:T(128)S(1)} %get-tuple-element.2), channel_id=1, replica_groups=mesh['wa'=4,'ha'=8] {'wa'}, use_global_device_ids=true, to_apply=%region_10.11 | all-reduce | flops 128 | bytes 1024 | tf_op jit(solution)/shard_map/psum | solution.py:108
  529.4 1.3 fusion.14
  (39 shorter events, 3.8 us)
Async XLA Ops:
  7.2 59.7 %all-gather.3.cloned.1.call-start = ((), (), s32[]{:S(2)}) async-start(), calls=%async_computation.2 | async-start | bytes 9437184 | tf_op jit(solution)/shard_map/all_gather | solution.py:47
  7.9 117.8 %all-reduce.2.cloned.1.call-start = ((), (), s32[]{:S(2)}) async-start(), calls=%async_computation.3 | async-start | bytes 2097152 | tf_op jit(solution)/shard_map/psum | solution.py:53
  73.6 198.4 %reduce-scatter.3.cloned.1.call-start = ((), (), s32[]{:S(2)}) async-start(), calls=%async_computation.4 | async-start | bytes 10485760 | tf_op jit(solution)/shard_map/reduce_scatter | solution.py:66
  97.7 1.2 copy-start
  97.7 22.2 %copy-start.2 = (s32[1024]{0:T(1024)S(1)}, s32[1024]{0:T(1024)}, u32[]{:S(2)}) copy-start(s32[1024]{0:T(1024)} %param.15) | copy-start | bytes 12292
  97.7 418.0 %reduce-scatter.5.cloned.1.call-start = ((), (), s32[]{:S(2)}) async-start(), calls=%async_computation.5 | async-start | bytes 18874368 | tf_op jit(solution)/shard_map/reduce_scatter | solution.py:100
  295.8 26.4 %collective-permute-start = (bf16[256,2048]{0,1:T(8,128)(2,1)S(1)}, bf16[256,2048]{0,1:T(8,128)(2,1)S(1)}, u32[]{:S(2)}, u32[]{:S(2)}) collective-permute-start(bf16[256,2048]{0,1:T(8,128)(2,1)S(1)} %bitcast.51), channel_id=1, source_target_pairs={{0,8},{8,16},{16,24},{24,0},{1,9},{9,17},{17,25},{25,1},{2,10},{10... | collective-permute-start | bytes 3145736 | tf_op jit(solution)/shard_map/ppermute | solution.py:95
  322.1 25.6 %collective-permute-start.1 = (bf16[256,2048]{0,1:T(8,128)(2,1)S(1)}, bf16[256,2048]{0,1:T(8,128)(2,1)}, u32[]{:S(2)}, u32[]{:S(2)}) collective-permute-start(bf16[256,2048]{0,1:T(8,128)(2,1)S(1)} %collective-permute-done), channel_id=1, source_target_pairs={{0,8},{8,16},{16,24},{24,0},{1,9},{9,17},{17,25},{25,1},{2,10},{10... | collective-permute-start | bytes 3145736 | tf_op jit(solution)/shard_map/ppermute | solution.py:95
  347.7 24.9 %collective-permute-start.2 = (bf16[256,2048]{0,1:T(8,128)(2,1)}, bf16[256,2048]{0,1:T(8,128)(2,1)}, u32[]{:S(2)}, u32[]{:S(2)}) collective-permute-start(bf16[256,2048]{0,1:T(8,128)(2,1)} %collective-permute-done.1), channel_id=1, source_target_pairs={{0,8},{8,16},{16,24},{24,0},{1,9},{9,17},{17,25},{25,1},{2,10},{10... | collective-permute-start | bytes 3145736 | tf_op jit(solution)/shard_map/ppermute | solution.py:95
  401.2 0.7 copy-start.3
  517.7 13.0 %copy-start.1 = (bf16[128,4096]{1,0:T(8,128)(2,1)}, bf16[128,4096]{1,0:T(8,128)(2,1)S(1)}, u32[]{:S(2)}) copy-start(bf16[128,4096]{1,0:T(8,128)(2,1)S(1)} %get-tuple-element.3) | copy-start | bytes 3145732
Sparse Core Ops, SparseCore 0:
  9.9 56.9 all-gather.2
  73.7 51.9 all-reduce.1
  128.1 143.8 reduce-scatter.2
  401.3 114.3 reduce-scatter.4
